TPU v7x, 32 devices: a whole 2x2x4 slice. The times are simulated.
32 devices in a mesh: seq: 4 (over x, core), dp: 8 (over z, y).
Axes of the slice: x: 2, y: 2, z: 4, core: 2. Of those that a mesh axis runs over, the one named last changes fastest.
Arguments:
- tokens: bfloat16 [8, 1280, 960], P('dp', 'seq'), may hold values from -6 to 6
- seg_ids: int32 [8, 1280], P('dp', 'seq'), may hold values from 0 to 4, as said below
- positions: int32 [8, 1280], P('dp', 'seq'), may hold values from 0 to 1279, as said below
- attn_gain: float32 [960], replicated, may hold values from 0.25 to 1.75
- w_query: bfloat16 [960, 960], replicated, may hold values from -0.1875 to 0.1875
- w_key: bfloat16 [960, 320], replicated, may hold values from -0.1875 to 0.1875
- w_value: bfloat16 [960, 320], replicated, may hold values from -0.1875 to 0.1875
- w_out: bfloat16 [960, 960], replicated, may hold values from -0.5 to 0.5
- ffn_gain: float32 [960], replicated, may hold values from 0.25 to 1.75
- w_gate: bfloat16 [960, 2560], P(None, 'seq'), may hold values from -0.1875 to 0.1875
- w_up: bfloat16 [960, 2560], P(None, 'seq'), may hold values from -0.1875 to 0.1875
- w_down: bfloat16 [2560, 960], P('seq'), may hold values from -0.125 to 0.125
- cotangent: bfloat16 [8, 1280, 960], P('dp', 'seq'), may hold values from -6 to 6
Outputs:
- output: bfloat16 [8, 1280, 960], P('dp', 'seq')
- input_grad: float32 [8, 1280, 960], P('dp', 'seq')
- attn_gain_grad: float32 [960], P('dp')
- w_query_grad: float32 [960, 960], P('dp')
- w_key_grad: float32 [960, 320], P('dp')
- w_value_grad: float32 [960, 320], P('dp')
- w_out_grad: float32 [960, 960], P('dp')
- ffn_gain_grad: float32 [960], P('dp')
- w_gate_grad: float32 [960, 2560], P('dp', 'seq')
- w_up_grad: float32 [960, 2560], P('dp', 'seq')
- w_down_grad: float32 [2560, 960], P('seq', 'dp')
Inputs may be any that keep to these rules, and one draw needn't show every extreme that they name: `seg_ids`: within a row the ids start at 0 and never fall. `positions`: A token's position counts the tokens before it in its document (0 at a document's first token).
All inputs are finite; a program needn't handle non-finite values.
Results may differ from a plain program's by a relative error of at most 0.025.
Values may be sent and summed in bfloat16 or wider, within the bound.
A program may use at most 256 MiB of HBM per device.

v0:
```python
import jax
import jax.numpy as jnp
from jax import lax
from jax.sharding import PartitionSpec as P

HEADS = 15
KV_HEADS = 5
HEAD_DIM = 64
EPSILON = 1e-05
THETA = 10000.0
MASKED = -1e30


def rope_tables(positions):
    half_dim = HEAD_DIM // 2
    frequency = THETA ** (-(jnp.arange(half_dim, dtype=jnp.float32) * 2.0 / HEAD_DIM))
    angles = positions.astype(jnp.float32)[..., None] * frequency
    return (jnp.cos(angles), jnp.sin(angles))


def rotate(values, cos_table, sin_table):
    half_dim = values.shape[-1] // 2
    first_half = values[..., :half_dim]
    second_half = values[..., half_dim:]
    cos_head = cos_table[..., None, :]
    sin_head = sin_table[..., None, :]
    return jnp.concatenate(
        [
            first_half * cos_head - second_half * sin_head,
            second_half * cos_head + first_half * sin_head,
        ],
        axis=-1,
    )


def norm_forward(residual, gain_vec):
    inverse = lax.rsqrt(jnp.mean(residual * residual, axis=-1, keepdims=True) + EPSILON)
    return ((residual * inverse * gain_vec).astype(jnp.bfloat16), inverse)


def norm_backward(residual, inverse, gain_vec, upstream):
    weighted = upstream * gain_vec
    inner_mean = jnp.mean(weighted * residual, axis=-1, keepdims=True)
    residual_grad = inverse * weighted - residual * (inverse * inverse * inverse) * inner_mean
    gain_grad = jnp.sum(upstream * residual * inverse, axis=(0, 1))
    return (residual_grad, gain_grad)


def masked_scores(queries, keys_all, allowed):
    raw_scores = jnp.einsum("qkgd,tkd->kgqt", queries, keys_all, preferred_element_type=jnp.float32)
    return jnp.where(allowed[None, None], raw_scores * HEAD_DIM ** (-0.5), MASKED)


def row_attend(operands):
    queries, keys_all, values_all, allowed = operands
    scores = masked_scores(queries, keys_all, allowed)
    row_max = jnp.max(scores, axis=-1, keepdims=True)
    shifted = jnp.exp(scores - row_max)
    row_total = jnp.sum(shifted, axis=-1, keepdims=True)
    probs_low = (shifted / row_total).astype(jnp.bfloat16)
    mixed_heads = jnp.einsum(
        "kgqt,tkd->qkgd", probs_low, values_all, preferred_element_type=jnp.float32
    )
    return (mixed_heads, row_max + jnp.log(row_total))


def row_backward(operands):
    queries, keys_all, values_all, allowed, log_total, mixed_grad = operands
    scores = masked_scores(queries, keys_all, allowed)
    weights_soft = jnp.exp(scores - log_total)
    probs_grad = jnp.einsum(
        "qkgd,tkd->kgqt", mixed_grad, values_all, preferred_element_type=jnp.float32
    )
    row_delta = jnp.sum(probs_grad * weights_soft, axis=-1, keepdims=True)
    score_grad = (weights_soft * (probs_grad - row_delta)).astype(jnp.bfloat16)
    score_scale = HEAD_DIM ** (-0.5)
    query_grad = (
        jnp.einsum("kgqt,tkd->qkgd", score_grad, keys_all, preferred_element_type=jnp.float32)
        * score_scale
    )
    key_grad = (
        jnp.einsum("kgqt,qkgd->tkd", score_grad, queries, preferred_element_type=jnp.float32)
        * score_scale
    )
    value_grad = jnp.einsum(
        "kgqt,qkgd->tkd",
        weights_soft.astype(jnp.bfloat16),
        mixed_grad,
        preferred_element_type=jnp.float32,
    )
    return (query_grad, key_grad, value_grad)


def on_device(
    tokens,
    seg_ids,
    positions,
    attn_gain,
    w_query,
    w_key,
    w_value,
    w_out,
    ffn_gain,
    w_gate,
    w_up,
    w_down,
    cotangent,
):
    row_count, shard_len, model_width = tokens.shape
    row_len = shard_len * lax.axis_size("seq")
    groups = HEADS // KV_HEADS
    kv_width = KV_HEADS * HEAD_DIM
    doc_all = lax.all_gather(seg_ids, "seq", axis=1, tiled=True)
    query_place = lax.axis_index("seq") * shard_len + jnp.arange(shard_len, dtype=jnp.int32)
    key_place = jnp.arange(row_len, dtype=jnp.int32)
    allowed = (seg_ids[:, :, None] == doc_all[:, None, :]) & (
        key_place[None, None, :] <= query_place[None, :, None]
    )
    cos_table, sin_table = rope_tables(positions)
    gate_mat, up_mat, down_mat = (
        lax.all_gather(w_gate, "seq", axis=1, tiled=True),
        lax.all_gather(w_up, "seq", axis=1, tiled=True),
        lax.all_gather(w_down, "seq", axis=0, tiled=True),
    )
    residual = tokens.astype(jnp.float32)
    kept_runs = []
    for repeat in range(2):
        normed, attn_inverse = norm_forward(residual, attn_gain)
        query_pre = jnp.einsum("rcd,de->rce", normed, w_query, preferred_element_type=jnp.float32)
        key_pre = jnp.einsum("rcd,de->rce", normed, w_key, preferred_element_type=jnp.float32)
        value_pre = jnp.einsum("rcd,de->rce", normed, w_value, preferred_element_type=jnp.float32)
        queries = rotate(
            query_pre.reshape(row_count, shard_len, HEADS, HEAD_DIM), cos_table, sin_table
        ).astype(jnp.bfloat16)
        keys_local = rotate(
            key_pre.reshape(row_count, shard_len, KV_HEADS, HEAD_DIM), cos_table, sin_table
        ).astype(jnp.bfloat16)
        joined = jnp.concatenate(
            [keys_local.reshape(row_count, shard_len, kv_width), value_pre.astype(jnp.bfloat16)],
            axis=-1,
        )
        joined_all = lax.all_gather(joined, "seq", axis=1, tiled=True)
        keys_all = joined_all[..., :kv_width].reshape(row_count, row_len, KV_HEADS, HEAD_DIM)
        values_all = joined_all[..., kv_width:].reshape(row_count, row_len, KV_HEADS, HEAD_DIM)
        grouped = queries.reshape(row_count, shard_len, KV_HEADS, groups, HEAD_DIM)
        mixed_heads, log_total = lax.map(row_attend, (grouped, keys_all, values_all, allowed))
        mixed_low = mixed_heads.reshape(row_count, shard_len, HEADS * HEAD_DIM).astype(jnp.bfloat16)
        after_attn = residual + jnp.einsum(
            "rce,ed->rcd", mixed_low, w_out, preferred_element_type=jnp.float32
        )
        normed_two, ffn_inverse = norm_forward(after_attn, ffn_gain)
        gate_pre = jnp.einsum(
            "rtd,df->rtf", normed_two, gate_mat, preferred_element_type=jnp.float32
        )
        up_pre = jnp.einsum("rtd,df->rtf", normed_two, up_mat, preferred_element_type=jnp.float32)
        ffn_hidden = (jax.nn.silu(gate_pre) * up_pre).astype(jnp.bfloat16)
        partial_sum = jnp.einsum(
            "rtf,fd->rtd", ffn_hidden, down_mat, preferred_element_type=jnp.float32
        )
        normed_rows, gate_pre, up_pre, ffn_out = (normed_two, gate_pre, up_pre, partial_sum)
        kept_runs.append(
            (
                residual,
                normed,
                attn_inverse,
                grouped,
                keys_all,
                values_all,
                log_total,
                mixed_low,
                after_attn,
                ffn_inverse,
                normed_rows,
                gate_pre,
                up_pre,
            )
        )
        residual = after_attn + ffn_out
    output = residual.astype(jnp.bfloat16)
    attn_gain_grad = jnp.zeros(attn_gain.shape, jnp.float32)
    ffn_gain_grad = jnp.zeros(ffn_gain.shape, jnp.float32)
    w_query_grad = jnp.zeros(w_query.shape, jnp.float32)
    w_key_grad = jnp.zeros(w_key.shape, jnp.float32)
    w_value_grad = jnp.zeros(w_value.shape, jnp.float32)
    w_out_grad = jnp.zeros(w_out.shape, jnp.float32)
    w_gate_grad = jnp.zeros(gate_mat.shape, jnp.float32)
    w_up_grad = jnp.zeros(up_mat.shape, jnp.float32)
    w_down_grad = jnp.zeros(down_mat.shape, jnp.float32)
    upstream = cotangent.astype(jnp.float32)
    for repeat in (1, 0):
        (
            residual,
            normed,
            attn_inverse,
            grouped,
            keys_all,
            values_all,
            log_total,
            mixed_low,
            after_attn,
            ffn_inverse,
            normed_rows,
            gate_pre,
            up_pre,
        ) = kept_runs[repeat]
        ffn_grad = upstream.astype(jnp.bfloat16)
        sigmoid_gate = jax.nn.sigmoid(gate_pre)
        silu_gate = jax.nn.silu(gate_pre)
        hidden = (silu_gate * up_pre).astype(jnp.bfloat16)
        w_down_grad = w_down_grad + jnp.einsum(
            "rtf,rtd->fd", hidden, ffn_grad, preferred_element_type=jnp.float32
        )
        hidden_grad = jnp.einsum(
            "rtd,fd->rtf", ffn_grad, down_mat, preferred_element_type=jnp.float32
        )
        gate_grad = (
            hidden_grad * up_pre * sigmoid_gate * (1.0 + gate_pre * (1.0 - sigmoid_gate))
        ).astype(jnp.bfloat16)
        up_grad = (hidden_grad * silu_gate).astype(jnp.bfloat16)
        w_gate_grad = w_gate_grad + jnp.einsum(
            "rtd,rtf->df", normed_rows, gate_grad, preferred_element_type=jnp.float32
        )
        w_up_grad = w_up_grad + jnp.einsum(
            "rtd,rtf->df", normed_rows, up_grad, preferred_element_type=jnp.float32
        )
        normed_two_grad = jnp.einsum(
            "rtf,df->rtd", gate_grad, gate_mat, preferred_element_type=jnp.float32
        ) + jnp.einsum("rtf,df->rtd", up_grad, up_mat, preferred_element_type=jnp.float32)
        after_grad, gain_two = norm_backward(after_attn, ffn_inverse, ffn_gain, normed_two_grad)
        after_grad = after_grad + upstream
        ffn_gain_grad = ffn_gain_grad + gain_two
        attn_grad = after_grad.astype(jnp.bfloat16)
        w_out_grad = w_out_grad + jnp.einsum(
            "rce,rcd->ed", mixed_low, attn_grad, preferred_element_type=jnp.float32
        )
        mixed_grad = jnp.einsum(
            "rcd,ed->rce", attn_grad, w_out, preferred_element_type=jnp.float32
        ).astype(jnp.bfloat16)
        mixed_grad = mixed_grad.reshape(row_count, shard_len, KV_HEADS, groups, HEAD_DIM)
        query_grad, key_grad, value_grad = lax.map(
            row_backward, (grouped, keys_all, values_all, allowed, log_total, mixed_grad)
        )
        joined_grad = jnp.concatenate(
            [
                key_grad.reshape(row_count, row_len, kv_width),
                value_grad.reshape(row_count, row_len, kv_width),
            ],
            axis=-1,
        )
        local_grad = lax.psum_scatter(
            joined_grad.astype(jnp.bfloat16), "seq", scatter_dimension=1, tiled=True
        ).astype(jnp.float32)
        key_back = rotate(
            local_grad[..., :kv_width].reshape(row_count, shard_len, KV_HEADS, HEAD_DIM),
            cos_table,
            -sin_table,
        )
        key_back = key_back.reshape(row_count, shard_len, kv_width).astype(jnp.bfloat16)
        value_back = local_grad[..., kv_width:].astype(jnp.bfloat16)
        query_back = rotate(
            query_grad.reshape(row_count, shard_len, HEADS, HEAD_DIM), cos_table, -sin_table
        )
        query_back = query_back.reshape(row_count, shard_len, HEADS * HEAD_DIM).astype(jnp.bfloat16)
        w_query_grad = w_query_grad + jnp.einsum(
            "rcd,rce->de", normed, query_back, preferred_element_type=jnp.float32
        )
        w_key_grad = w_key_grad + jnp.einsum(
            "rcd,rce->de", normed, key_back, preferred_element_type=jnp.float32
        )
        w_value_grad = w_value_grad + jnp.einsum(
            "rcd,rce->de", normed, value_back, preferred_element_type=jnp.float32
        )
        normed_grad = jnp.einsum(
            "rce,de->rcd", query_back, w_query, preferred_element_type=jnp.float32
        )
        normed_grad = normed_grad + jnp.einsum(
            "rce,de->rcd", key_back, w_key, preferred_element_type=jnp.float32
        )
        normed_grad = normed_grad + jnp.einsum(
            "rce,de->rcd", value_back, w_value, preferred_element_type=jnp.float32
        )
        residual_grad, gain_one = norm_backward(residual, attn_inverse, attn_gain, normed_grad)
        attn_gain_grad = attn_gain_grad + gain_one
        upstream = residual_grad + after_grad
    w_gate_grad, w_up_grad, w_down_grad = (
        lax.psum_scatter(
            w_gate_grad.astype(jnp.bfloat16), "seq", scatter_dimension=1, tiled=True
        ).astype(jnp.float32),
        lax.psum_scatter(
            w_up_grad.astype(jnp.bfloat16), "seq", scatter_dimension=1, tiled=True
        ).astype(jnp.float32),
        lax.psum_scatter(
            w_down_grad.astype(jnp.bfloat16), "seq", scatter_dimension=0, tiled=True
        ).astype(jnp.float32),
    )
    shards = (
        lax.psum_scatter(attn_gain_grad, "dp", scatter_dimension=0, tiled=True),
        lax.psum_scatter(w_query_grad, "dp", scatter_dimension=0, tiled=True),
        lax.psum_scatter(w_key_grad, "dp", scatter_dimension=0, tiled=True),
        lax.psum_scatter(w_value_grad, "dp", scatter_dimension=0, tiled=True),
        lax.psum_scatter(w_out_grad, "dp", scatter_dimension=0, tiled=True),
        lax.psum_scatter(ffn_gain_grad, "dp", scatter_dimension=0, tiled=True),
        lax.psum_scatter(w_gate_grad, "dp", scatter_dimension=0, tiled=True),
        lax.psum_scatter(w_up_grad, "dp", scatter_dimension=0, tiled=True),
        lax.psum_scatter(w_down_grad, "dp", scatter_dimension=1, tiled=True),
    )
    attn_sums = (
        lax.psum(shards[0].astype(jnp.bfloat16), "seq").astype(jnp.float32),
        lax.psum(shards[1].astype(jnp.bfloat16), "seq").astype(jnp.float32),
        lax.psum(shards[2].astype(jnp.bfloat16), "seq").astype(jnp.float32),
        lax.psum(shards[3].astype(jnp.bfloat16), "seq").astype(jnp.float32),
        lax.psum(shards[4].astype(jnp.bfloat16), "seq").astype(jnp.float32),
        lax.psum(shards[5].astype(jnp.bfloat16), "seq").astype(jnp.float32),
    )
    return (
        output,
        upstream,
        attn_sums[0],
        attn_sums[1],
        attn_sums[2],
        attn_sums[3],
        attn_sums[4],
        attn_sums[5],
        shards[6],
        shards[7],
        shards[8],
    )


def solution(mesh):
    in_specs = (
        P("dp", "seq", None),
        P("dp", "seq"),
        P("dp", "seq"),
        P(),
        P(),
        P(),
        P(),
        P(),
        P(),
        P(None, "seq"),
        P(None, "seq"),
        P("seq", None),
        P("dp", "seq", None),
    )
    out_specs = (
        P("dp", "seq", None),
        P("dp", "seq", None),
        P("dp"),
        P("dp", None),
        P("dp", None),
        P("dp", None),
        P("dp", None),
        P("dp"),
        P("dp", "seq"),
        P("dp", "seq"),
        P("seq", "dp"),
    )
    return jax.shard_map(
        on_device, mesh=mesh, in_specs=in_specs, out_specs=out_specs, check_vma=False
    )
```

profile of v0, /device:TPU:0, one launch (start us, length us, event | category | flops | bytes accessed | tf_op | source)
XLA Modules:
  0.0 1120.8 jit_solution(3167693406144594181)
XLA Ops:
  45.4 13.7 %fusion.120 = (f32[5,3,320]{2,1,0:T(4,128)S(1)}, f32[5,3,320,1280]{3,2,1,0:T(8,128)}) fusion(bf16[1280,5,64,1]{0,2,3,1:T(8,128)(2,1)} %bitcast.365, bf16[320,5,3,32]{0,3,2,1:T(8,128)(2,1)} %bitcast.385, bf16[320,5,3,32]{0,3,2,1:T(8,128)(2,1)} %bitcast.383, pred[320,1280]{1,0:T(8,128)(4,1)S(1)} %fusion.36), kind=kOutput, calls=%fused_computation.230 | convolution fusion | flops 806088000 | bytes 26438400 | tf_op jit(solution)/shard_map/while/body/eval_jaxpr/qkgd,tkd->kgqt/dot_general | solution.py:50
  59.2 12.1 %fusion.6 = f32[5,3,320]{2,1,0:T(4,128)} fusion(f32[5,3,320,1280]{3,2,1,0:T(8,128)} %get-tuple-element.172, f32[5,3,320]{2,1,0:T(4,128)S(1)} %get-tuple-element.171), kind=kLoop, calls=%fused_computation.18 | loop fusion | flops 12283200 | bytes 24614400 | tf_op jit(solution)/shard_map/while/body/eval_jaxpr/reduce_sum | solution.py:59
  92.2 25.8 %all-gather.10.cloned.1.call-done = bf16[960,2560]{1,0:T(8,128)(2,1)} async-done(((bf16[960,640]{1,0:T(8,128)(2,1)}), bf16[960,2560]{1,0:T(8,128)(2,1)}) %all-gather.10.cloned.1.call-update) | async-done | bytes 4915216 | tf_op jit(solution)/shard_map/all_gather | solution.py:122
  125.8 32.2 %all-gather.12.cloned.1.call-done = bf16[2560,960]{0,1:T(8,128)(2,1)} async-done(((bf16[640,960]{0,1:T(8,128)(2,1)}), bf16[2560,960]{0,1:T(8,128)(2,1)}) %all-gather.12.cloned.1.call-update) | async-done | bytes 4915216 | tf_op jit(solution)/shard_map/all_gather | solution.py:123
  172.3 16.2 %all-gather.14.cloned.1.call-done = bf16[1,1280,640]{2,1,0:T(8,128)(2,1)} async-done(((bf16[1,320,640]{2,1,0:T(8,128)(2,1)}), bf16[1,1280,640]{2,1,0:T(8,128)(2,1)}) %all-gather.14.cloned.1.call-update) | async-done | bytes 1638416 | tf_op jit(solution)/shard_map/all_gather | solution.py:142
  194.8 12.4 %fusion.121 = (f32[5,3,320]{2,1,0:T(4,128)}, f32[5,3,320,1280]{3,2,1,0:T(8,128)}) fusion(bf16[1280,5,64,1]{0,2,3,1:T(8,128)(2,1)S(1)} %bitcast.367, bf16[320,5,3,32]{0,3,2,1:T(8,128)(2,1)} %bitcast.389, bf16[320,5,3,32]{0,3,2,1:T(8,128)(2,1)} %bitcast.387, pred[320,1280]{1,0:T(8,128)(4,1)S(1)} %copy-done.26), kind=kOutput, calls=%fused_computation.231 | convolution fusion | flops 806088000 | bytes 26438400 | tf_op jit(solution)/shard_map/while/body/eval_jaxpr/qkgd,tkd->kgqt/dot_general | solution.py:50
  207.2 12.3 %fusion.7 = f32[5,3,320]{2,1,0:T(4,128)S(1)} fusion(f32[5,3,320,1280]{3,2,1,0:T(8,128)} %get-tuple-element.180, f32[5,3,320]{2,1,0:T(4,128)} %get-tuple-element.179), kind=kLoop, calls=%fused_computation.19 | loop fusion | flops 12283200 | bytes 24614400 | tf_op jit(solution)/shard_map/while/body/eval_jaxpr/reduce_sum | solution.py:59
  252.1 9.8 fusion.28
  262.0 19.4 %fusion.3 = (f32[5,3,320]{2,1,0:T(4,128)S(1)}, f32[5,1280,320,3]{1,2,3,0:T(8,128)}) fusion(f32[5,3,320,1280]{3,2,1,0:T(8,128)} %get-tuple-element.180, f32[5,3,320]{2,1,0:T(4,128)S(1)} %copy-done.66, bf16[1280,5,64,1]{0,2,3,1:T(8,128)(2,1)S(1)} %bitcast.394, bf16[320,5,3,64]{0,3,2,1:T(8,128)(2,1)S(1)} %bitcast.372), kind=kOutput, calls=%fused_computation.7 | convolution fusion | flops 804859200 | bytes 50624000 | tf_op jit(solution)/shard_map/while/body/eval_jaxpr/qkgd,tkd->kgqt/dot_general | solution.py:71
  281.4 16.4 %fusion.5 = bf16[5,3,320,1280]{3,2,1,0:T(8,128)(2,1)S(1)} fusion(f32[5,1280,320,3]{1,2,3,0:T(8,128)} %get-tuple-element.185, f32[5,3,320,1280]{3,2,1,0:T(8,128)} %get-tuple-element.180, f32[5,3,320]{2,1,0:T(4,128)S(1)} %get-tuple-element.184, f32[5,3,320]{2,1,0:T(4,128)S(1)} %copy-done.66), kind=kLoop, calls=%fused_computation.9 | loop fusion | flops 24576000 | bytes 61478400 | tf_op jit(solution)/shard_map/while/body/eval_jaxpr/convert_element_type | solution.py:75
  324.9 18.4 %reduce-scatter.33.cloned.1.call-done = bf16[320,640]{1,0:T(8,128)(2,1)} async-done(((bf16[1280,640]{1,0:T(8,128)(2,1)}), bf16[320,640]{1,0:T(8,128)(2,1)}) %reduce-scatter.33.cloned.1.call-update) | async-done | bytes 409616
  371.9 9.8 fusion.31
  381.7 19.4 %fusion = (f32[5,3,320]{2,1,0:T(4,128)S(1)}, f32[5,1280,320,3]{1,2,3,0:T(8,128)}) fusion(f32[5,3,320,1280]{3,2,1,0:T(8,128)} %get-tuple-element.172, f32[5,3,320]{2,1,0:T(4,128)S(1)} %copy-done.65, bf16[1280,5,64,1]{0,2,3,1:T(8,128)(2,1)S(1)} %bitcast.392, bf16[320,5,3,64]{0,3,2,1:T(8,128)(2,1)S(1)} %bitcast.374), kind=kOutput, calls=%fused_computation.2 | convolution fusion | flops 804859200 | bytes 50624000 | tf_op jit(solution)/shard_map/while/body/eval_jaxpr/qkgd,tkd->kgqt/dot_general | solution.py:71
  401.1 16.4 %fusion.2 = bf16[5,3,320,1280]{3,2,1,0:T(8,128)(2,1)S(1)} fusion(f32[5,1280,320,3]{1,2,3,0:T(8,128)} %get-tuple-element.189, f32[5,3,320,1280]{3,2,1,0:T(8,128)} %get-tuple-element.172, f32[5,3,320]{2,1,0:T(4,128)S(1)} %get-tuple-element.188, f32[5,3,320]{2,1,0:T(4,128)S(1)} %copy-done.65), kind=kLoop, calls=%fused_computation.4 | loop fusion | flops 24576000 | bytes 61478400 | tf_op jit(solution)/shard_map/while/body/eval_jaxpr/convert_element_type | solution.py:75
  437.8 9.0 convolution_multiply_fusion
  533.5 134.0 %all-reduce.15 = (bf16[960]{0:T(1024)(128)(2,1)S(1)}, bf16[960,320]{0,1:T(8,128)(2,1)S(1)}, bf16[960,320]{0,1:T(8,128)(2,1)}, bf16[960]{0:T(1024)(128)(2,1)S(1)}) all-reduce(f32[960]{0:T(1024)S(1)} %add.284, f32[960,320]{0,1:T(8,128)} %convolution_add_fusion.5, ...), channel_id=4, replica_groups=mesh['seq'=4,'dp'=8] {'dp'}, use_global_device_ids=true, to_apply=%region_18.19.clone | all-reduce | flops 616320 | bytes 3697920
  670.9 23.2 %reduce-scatter.31.cloned.1.call-done = f32[120,960]{1,0:T(8,128)} async-done(((f32[960,960]{1,0:T(8,128)}), f32[120,960]{1,0:T(8,128)}) %reduce-scatter.31.cloned.1.call-update) | async-done | bytes 460816 | tf_op jit(solution)/shard_map/reduce_scatter | solution.py:301
  696.0 51.7 %reduce-scatter.37.cloned.1.call-done = bf16[640,960]{1,0:T(8,128)(2,1)} async-done(((bf16[2560,960]{1,0:T(8,128)(2,1)}), bf16[640,960]{1,0:T(8,128)(2,1)}) %reduce-scatter.37.cloned.1.call-update) | async-done | bytes 1228816
  753.0 48.8 %reduce-scatter.39.cloned.1.call-done = bf16[640,960]{1,0:T(8,128)(2,1)} async-done(((bf16[2560,960]{1,0:T(8,128)(2,1)}), bf16[640,960]{1,0:T(8,128)(2,1)}) %reduce-scatter.39.cloned.1.call-update) | async-done | bytes 1228816
  807.1 48.4 %reduce-scatter.41.cloned.1.call-done = bf16[640,960]{1,0:T(8,128)(2,1)} async-done(((bf16[2560,960]{1,0:T(8,128)(2,1)}), bf16[640,960]{1,0:T(8,128)(2,1)}) %reduce-scatter.41.cloned.1.call-update) | async-done | bytes 1228816
  877.4 15.7 %all-reduce.14.cloned.1.call-done = (bf16[120,960]{1,0:T(8,128)(2,1)}, bf16[120,320]{0,1:T(8,128)(2,1)}, bf16[120,320]{0,1:T(8,128)(2,1)}, bf16[120,960]{1,0:T(8,128)(2,1)}) async-done(((bf16[120,960]{1,0:T(8,128)(2,1)}, bf16[120,320]{0,1:T(8,128)(2,1)}, bf16[120,320]{0,1:T(8,128)(2,1)}, bf16[120,960]{1,0:T(8,128)(2,1)}), (bf16[120,960]{1,0:T(8,128)(2,1)}, bf16[120,320]{0,1:T(8,128)(2,1)}, ...) | async-done | bytes 614416 | tf_op jit(solution)/shard_map/psum | solution.py:309
  899.8 67.6 %reduce-scatter.43.cloned.1.call-done = f32[120,640]{1,0:T(8,128)} async-done(((f32[960,640]{1,0:T(8,128)}), f32[120,640]{1,0:T(8,128)}) %reduce-scatter.43.cloned.1.call-update) | async-done | bytes 307216
  967.4 73.3 %reduce-scatter.45.cloned.1.call-done = f32[120,640]{1,0:T(8,128)} async-done(((f32[960,640]{1,0:T(8,128)}), f32[120,640]{1,0:T(8,128)}) %reduce-scatter.45.cloned.1.call-update) | async-done | bytes 307216
  1040.6 73.2 %reduce-scatter.47.cloned.1.call-done = f32[640,120]{0,1:T(8,128)} async-done(((f32[640,960]{0,1:T(8,128)}), f32[640,120]{0,1:T(8,128)}) %reduce-scatter.47.cloned.1.call-update) | async-done | bytes 307216
  (394 shorter events, 324.2 us)
Async XLA Ops:
  7.2 74.2 %copy-start = (bf16[960,960]{1,0:T(8,128)(2,1)S(1)}, bf16[960,960]{1,0:T(8,128)(2,1)}, u32[]{:S(2)}) copy-start(bf16[960,960]{1,0:T(8,128)(2,1)} %param.20) | copy-start | bytes 5529604
  7.2 30.5 %all-gather.6.cloned.1.call-start = ((), (), s32[]{:S(2)}) async-start(), calls=%async_computation.10 | async-start | bytes 2048000 | tf_op jit(solution)/shard_map/all_gather | solution.py:142
  13.4 157.7 %copy-start.35 = (f32[320,32]{0,1:T(8,128)}, f32[320,32]{0,1:T(8,128)S(1)}, u32[]{:S(2)}) copy-start(f32[320,32]{0,1:T(8,128)S(1)} %get-tuple-element.162) | copy-start | bytes 122884
  14.7 70.1 %all-gather.8.cloned.1.call-start = ((), (), s32[]{:S(2)}) async-start(), calls=%async_computation.11 | async-start | bytes 6144000 | tf_op jit(solution)/shard_map/all_gather | solution.py:121
  15.4 102.6 %all-gather.10.cloned.1.call-start = ((), (), s32[]{:S(2)}) async-start(), calls=%async_computation.12 | async-start | bytes 6144000 | tf_op jit(solution)/shard_map/all_gather | solution.py:122
  16.2 141.8 %all-gather.12.cloned.1.call-start = ((), (), s32[]{:S(2)}) async-start(), calls=%async_computation.13 | async-start | bytes 6144000 | tf_op jit(solution)/shard_map/all_gather | solution.py:123
  16.7 171.8 %all-gather.14.cloned.1.call-start = ((), (), s32[]{:S(2)}) async-start(), calls=%async_computation.14 | async-start | bytes 2048000 | tf_op jit(solution)/shard_map/all_gather | solution.py:142
  92.2 65.8 %copy-start.13 = (f32[1,320,960]{2,1,0:T(8,128)S(1)}, f32[1,320,960]{2,1,0:T(8,128)}, u32[]{:S(2)}) copy-start(f32[1,320,960]{2,1,0:T(8,128)} %copy-done.12) | copy-start | bytes 3686404
  168.4 174.9 %reduce-scatter.33.cloned.1.call-start = ((), (), s32[]{:S(2)}) async-start(), calls=%async_computation.17 | async-start | bytes 2048000
  281.4 16.4 %copy-start.40 = (bf16[1,320,15,32]{1,3,2,0:T(8,128)(2,1)S(1)}, bf16[1,320,15,32]{1,3,2,0:T(8,128)(2,1)}, u32[]{:S(2)}) copy-start(bf16[1,320,15,32]{1,3,2,0:T(8,128)(2,1)} %get-tuple-element.144) | copy-start | bytes 921604
  281.4 16.4 %copy-start.41 = (bf16[1,320,15,32]{1,3,2,0:T(8,128)(2,1)S(1)}, bf16[1,320,15,32]{1,3,2,0:T(8,128)(2,1)}, u32[]{:S(2)}) copy-start(bf16[1,320,15,32]{1,3,2,0:T(8,128)(2,1)} %get-tuple-element.145) | copy-start | bytes 921604
  314.5 201.0 %reduce-scatter.35.cloned.1.call-start = ((), (), s32[]{:S(2)}) async-start(), calls=%async_computation.18 | async-start | bytes 2048000
  324.9 28.7 %copy-start.47 = (bf16[1,320,15,64]{1,3,2,0:T(8,128)(2,1)}, bf16[1,320,15,64]{1,3,2,0:T(8,128)(2,1)S(1)}, u32[]{:S(2)}) copy-start(bf16[1,320,15,64]{1,3,2,0:T(8,128)(2,1)S(1)} %maximum_convert_fusion) | copy-start | bytes 1843204
  401.1 16.4 %copy-start.38 = (bf16[1,320,15,32]{1,3,2,0:T(8,128)(2,1)S(1)}, bf16[1,320,15,32]{1,3,2,0:T(8,128)(2,1)}, u32[]{:S(2)}) copy-start(bf16[1,320,15,32]{1,3,2,0:T(8,128)(2,1)} %get-tuple-element.146) | copy-start | bytes 921604
  401.1 16.4 %copy-start.39 = (bf16[1,320,15,32]{1,3,2,0:T(8,128)(2,1)S(1)}, bf16[1,320,15,32]{1,3,2,0:T(8,128)(2,1)}, u32[]{:S(2)}) copy-start(bf16[1,320,15,32]{1,3,2,0:T(8,128)(2,1)} %get-tuple-element.147) | copy-start | bytes 921604
  434.3 234.9 %reduce-scatter.29.cloned.1.call-start = ((), (), s32[]{:S(2)}) async-start(), calls=%async_computation.15 | async-start | bytes 4423680 | tf_op jit(solution)/shard_map/reduce_scatter | solution.py:298
  451.5 242.6 %reduce-scatter.31.cloned.1.call-start = ((), (), s32[]{:S(2)}) async-start(), calls=%async_computation.16 | async-start | bytes 4423680 | tf_op jit(solution)/shard_map/reduce_scatter | solution.py:301
  457.6 290.0 %reduce-scatter.37.cloned.1.call-start = ((), (), s32[]{:S(2)}) async-start(), calls=%async_computation.19 | async-start | bytes 6553600
  475.1 326.6 %reduce-scatter.39.cloned.1.call-start = ((), (), s32[]{:S(2)}) async-start(), calls=%async_computation.20 | async-start | bytes 6553600
  492.3 363.2 %reduce-scatter.41.cloned.1.call-start = ((), (), s32[]{:S(2)}) async-start(), calls=%async_computation.21 | async-start | bytes 6553600
  509.6 383.5 %all-reduce.14.cloned.1.call-start = ((), (), s32[]{:S(2)}) async-start(), calls=%async_computation.25 | async-start | bytes 1310720 | tf_op jit(solution)/shard_map/psum | solution.py:309
  695.9 271.5 %reduce-scatter.43.cloned.1.call-start = ((), (), s32[]{:S(2)}) async-start(), calls=%async_computation.22 | async-start | bytes 2764800
  752.9 287.7 %reduce-scatter.45.cloned.1.call-start = ((), (), s32[]{:S(2)}) async-start(), calls=%async_computation.23 | async-start | bytes 2764800
  807.1 306.8 %reduce-scatter.47.cloned.1.call-start = ((), (), s32[]{:S(2)}) async-start(), calls=%async_computation.24 | async-start | bytes 2764800
  (97 other events, 418.2 us)
Sparse Core Ops, SparseCore 0:
  14.8 22.8 all-gather.5
  39.3 38.5 all-gather.7
  79.4 38.5 all-gather.9
  119.4 38.5 all-gather.11
  168.5 20.0 all-gather.13
  314.7 28.5 reduce-scatter.32
  434.4 28.5 reduce-scatter.34
  466.7 89.4 reduce-scatter.28
  560.3 133.7 reduce-scatter.30
  696.5 51.0 reduce-scatter.36
  750.4 51.3 reduce-scatter.38
  804.1 51.3 reduce-scatter.40
  858.8 34.2 all-reduce.13
  897.6 69.7 reduce-scatter.42
  971.9 68.7 reduce-scatter.44
  1045.1 68.6 reduce-scatter.46
where the time goes:
time: 1130 us; the launch traced here: 1120 us
  waiting for transfers between devices  501 us (44%)
  matrix products  243 us (22%)
  blocking collectives  147 us (13%)
  local copies, waits for them, and re-layouts  111 us (10%)
  other arithmetic  100 us (9%)
  between operations  17.3 us (2%)
    unnamed x24, waiting for transfers between devices  383 us
    unnamed x2, blocking collectives  141 us
    unnamed x233, local copies, waits for them, and re-layouts  88.9 us
    dot_general x2, matrix products, row_backward(): jnp.einsum('qkgd,tkd->kgqt', mixed_grad, values_all, preferred_element_ty...  38.8 us
    convert_element_type x2, other arithmetic, row_backward(): score_grad = (weights_soft * (probs_grad - row_delta)).astype(jnp.bfloat16)  32.7 us
    all_gather x1, waiting for transfers between devices, on_device(): lax.all_gather(w_down, 'seq', axis=0, tiled=True)  32.2 us
    dot_general x2, matrix products, masked_scores(): jnp.einsum('qkgd,tkd->kgqt', queries, keys_all, preferred_element_type=jn...  26.1 us
    all_gather x1, waiting for transfers between devices, on_device(): lax.all_gather(w_up, 'seq', axis=1, tiled=True)  25.8 us
  transfers between devices with their start and end apart: 16, of which 13 were waited for; matrix products, arithmetic and copies ran while one was open for 19% of the time, Pallas kernels for 0%

commit v1 on v0

--- a/solution.py
+++ b/solution.py
@@ -119,7 +119,9 @@
     cos_table, sin_table = rope_tables(positions)
     gate_mat, up_mat, down_mat = (
         lax.all_gather(w_gate, "seq", axis=1, tiled=True),
-        lax.all_gather(w_up, "seq", axis=1, tiled=True),
+        jnp.concatenate(
+            lax.all_to_all(jnp.stack([w_up] * lax.axis_size("seq")), "seq", 0, 0), axis=1
+        ),
         lax.all_gather(w_down, "seq", axis=0, tiled=True),
     )
     residual = tokens.astype(jnp.float32)

time: 1130 us -> 1150 us (1.018)
  blocking collectives: 147 us -> 221 us
  waiting for transfers between devices: 501 us -> 439 us
    unnamed x2, blocking collectives: 141 us -> 215 us
    all_gather x1, waiting for transfers between devices: 32.2 us -> 0.01 us  [on_device(): lax.all_gather(w_down, 'seq', axis=0, tiled=True)]
    all_gather x1 -> x0, waiting for transfers between devices: 25.8 us -> none  [on_device(): lax.all_gather(w_up, 'seq', axis=1, tiled=True)]
    unnamed x233 -> x235, local copies, waits for them, and re-layouts: 88.9 us -> 89.6 us
    unnamed x24 -> x23, waiting for transfers between devices: 383 us -> 383 us
  transfers between devices with their start and end apart: 16 -> 16, of which waited for: 13 -> 10; matrix products, arithmetic and copies ran while one was open for 19% -> 19% of each run, Pallas kernels for 0% -> 0%
where the time goes in v1:
time: 1150 us; the launch traced here: 1140 us
  waiting for transfers between devices  439 us (38%)
  matrix products  239 us (21%)
  blocking collectives  221 us (19%)
  local copies, waits for them, and re-layouts  122 us (11%)
  other arithmetic  101 us (9%)
  between operations  17.3 us (2%)
    unnamed x23, waiting for transfers between devices  383 us
    unnamed x2, blocking collectives  215 us
    unnamed x235, local copies, waits for them, and re-layouts  89.6 us
    dot_general x2, matrix products, row_backward(): jnp.einsum('qkgd,tkd->kgqt', mixed_grad, values_all, preferred_element_ty...  38.8 us
    convert_element_type x2, other arithmetic, row_backward(): score_grad = (weights_soft * (probs_grad - row_delta)).astype(jnp.bfloat16)  32.9 us
    dot_general x2, matrix products, masked_scores(): jnp.einsum('qkgd,tkd->kgqt', queries, keys_all, preferred_element_type=jn...  25.9 us
    reduce_sum x2, other arithmetic, row_attend(): row_total = jnp.sum(shifted, axis=-1, keepdims=True)  24.5 us
    reduce_scatter x1, waiting for transfers between devices, on_device(): lax.psum_scatter(w_out_grad, 'dp', scatter_dimension=0, tiled=True)  23.9 us
  transfers between devices with their start and end apart: 16, of which 10 were waited for; matrix products, arithmetic and copies ran while one was open for 19% of the time, Pallas kernels for 0%

profile of v1, /device:TPU:0, one launch (start us, length us, event | category | flops | bytes accessed | tf_op | source)
XLA Modules:
  0.0 1144.5 jit_solution(10415840720253636638)
XLA Ops:
  34.4 81.0 %all-reduce = s32[1280]{0:T(1024)S(1)} all-reduce(s32[1280]{0:T(1024)S(1)} %dynamic-update-slice), channel_id=1, replica_groups=mesh['seq'=4,'dp'=8] {'seq'}, use_global_device_ids=true, to_apply=%add | all-reduce | flops 1280 | bytes 10240
  124.2 13.6 %fusion.120 = (f32[5,3,320]{2,1,0:T(4,128)S(1)}, f32[5,3,320,1280]{3,2,1,0:T(8,128)}) fusion(bf16[1280,5,64,1]{0,2,3,1:T(8,128)(2,1)} %bitcast.368, bf16[320,5,3,32]{0,3,2,1:T(8,128)(2,1)} %bitcast.396, bf16[320,5,3,32]{0,3,2,1:T(8,128)(2,1)} %bitcast.394, pred[320,1280]{1,0:T(8,128)(4,1)S(1)} %fusion.36), kind=kOutput, calls=%fused_computation.230 | convolution fusion | flops 806088000 | bytes 26438400 | tf_op jit(solution)/shard_map/while/body/eval_jaxpr/qkgd,tkd->kgqt/dot_general | solution.py:50
  137.8 12.0 %fusion.6 = f32[5,3,320]{2,1,0:T(4,128)} fusion(f32[5,3,320,1280]{3,2,1,0:T(8,128)} %get-tuple-element.172, f32[5,3,320]{2,1,0:T(4,128)S(1)} %get-tuple-element.171), kind=kLoop, calls=%fused_computation.18 | loop fusion | flops 12283200 | bytes 24614400 | tf_op jit(solution)/shard_map/while/body/eval_jaxpr/reduce_sum | solution.py:59
  194.7 16.1 %all-gather.11.cloned.1.call-done = bf16[1,1280,640]{2,1,0:T(8,128)(2,1)} async-done(((bf16[1,320,640]{2,1,0:T(8,128)(2,1)}), bf16[1,1280,640]{2,1,0:T(8,128)(2,1)}) %all-gather.11.cloned.1.call-update) | async-done | bytes 1638416 | tf_op jit(solution)/shard_map/all_gather | solution.py:144
  217.0 12.3 %fusion.121 = (f32[5,3,320]{2,1,0:T(4,128)}, f32[5,3,320,1280]{3,2,1,0:T(8,128)}) fusion(bf16[1280,5,64,1]{0,2,3,1:T(8,128)(2,1)S(1)} %bitcast.370, bf16[320,5,3,32]{0,3,2,1:T(8,128)(2,1)} %bitcast.400, bf16[320,5,3,32]{0,3,2,1:T(8,128)(2,1)} %bitcast.398, pred[320,1280]{1,0:T(8,128)(4,1)S(1)} %copy-done.26), kind=kOutput, calls=%fused_computation.231 | convolution fusion | flops 806088000 | bytes 26438400 | tf_op jit(solution)/shard_map/while/body/eval_jaxpr/qkgd,tkd->kgqt/dot_general | solution.py:50
  229.4 12.5 %fusion.7 = f32[5,3,320]{2,1,0:T(4,128)S(1)} fusion(f32[5,3,320,1280]{3,2,1,0:T(8,128)} %get-tuple-element.180, f32[5,3,320]{2,1,0:T(4,128)} %get-tuple-element.179), kind=kLoop, calls=%fused_computation.19 | loop fusion | flops 12283200 | bytes 24614400 | tf_op jit(solution)/shard_map/while/body/eval_jaxpr/reduce_sum | solution.py:59
  274.3 9.8 fusion.28
  284.1 19.4 %fusion.3 = (f32[5,3,320]{2,1,0:T(4,128)S(1)}, f32[5,1280,320,3]{1,2,3,0:T(8,128)}) fusion(f32[5,3,320,1280]{3,2,1,0:T(8,128)} %get-tuple-element.180, f32[5,3,320]{2,1,0:T(4,128)S(1)} %copy-done.67, bf16[1280,5,64,1]{0,2,3,1:T(8,128)(2,1)S(1)} %bitcast.405, bf16[320,5,3,64]{0,3,2,1:T(8,128)(2,1)S(1)} %bitcast.375), kind=kOutput, calls=%fused_computation.7 | convolution fusion | flops 804859200 | bytes 50624000 | tf_op jit(solution)/shard_map/while/body/eval_jaxpr/qkgd,tkd->kgqt/dot_general | solution.py:71
  303.6 16.4 %fusion.5 = bf16[5,3,320,1280]{3,2,1,0:T(8,128)(2,1)S(1)} fusion(f32[5,1280,320,3]{1,2,3,0:T(8,128)} %get-tuple-element.185, f32[5,3,320,1280]{3,2,1,0:T(8,128)} %get-tuple-element.180, f32[5,3,320]{2,1,0:T(4,128)S(1)} %get-tuple-element.184, f32[5,3,320]{2,1,0:T(4,128)S(1)} %copy-done.67), kind=kLoop, calls=%fused_computation.9 | loop fusion | flops 24576000 | bytes 61478400 | tf_op jit(solution)/shard_map/while/body/eval_jaxpr/convert_element_type | solution.py:75
  338.1 8.6 convolution_multiply_fusion.1
  347.1 18.4 %reduce-scatter.33.cloned.1.call-done = bf16[320,640]{1,0:T(8,128)(2,1)} async-done(((bf16[1280,640]{1,0:T(8,128)(2,1)}), bf16[320,640]{1,0:T(8,128)(2,1)}) %reduce-scatter.33.cloned.1.call-update) | async-done | bytes 409616
  394.7 9.8 fusion.31
  404.6 19.4 %fusion = (f32[5,3,320]{2,1,0:T(4,128)S(1)}, f32[5,1280,320,3]{1,2,3,0:T(8,128)}) fusion(f32[5,3,320,1280]{3,2,1,0:T(8,128)} %get-tuple-element.172, f32[5,3,320]{2,1,0:T(4,128)S(1)} %copy-done.66, bf16[1280,5,64,1]{0,2,3,1:T(8,128)(2,1)S(1)} %bitcast.403, bf16[320,5,3,64]{0,3,2,1:T(8,128)(2,1)S(1)} %bitcast.377), kind=kOutput, calls=%fused_computation.2 | convolution fusion | flops 804859200 | bytes 50624000 | tf_op jit(solution)/shard_map/while/body/eval_jaxpr/qkgd,tkd->kgqt/dot_general | solution.py:71
  424.0 16.5 %fusion.2 = bf16[5,3,320,1280]{3,2,1,0:T(8,128)(2,1)S(1)} fusion(f32[5,1280,320,3]{1,2,3,0:T(8,128)} %get-tuple-element.189, f32[5,3,320,1280]{3,2,1,0:T(8,128)} %get-tuple-element.172, f32[5,3,320]{2,1,0:T(4,128)S(1)} %get-tuple-element.188, f32[5,3,320]{2,1,0:T(4,128)S(1)} %copy-done.66), kind=kLoop, calls=%fused_computation.4 | loop fusion | flops 24576000 | bytes 61478400 | tf_op jit(solution)/shard_map/while/body/eval_jaxpr/convert_element_type | solution.py:75
  460.9 9.0 convolution_multiply_fusion
  556.5 133.7 %all-reduce.15 = (bf16[960]{0:T(1024)(128)(2,1)S(1)}, bf16[960,320]{0,1:T(8,128)(2,1)S(1)}, bf16[960,320]{0,1:T(8,128)(2,1)}, bf16[960]{0:T(1024)(128)(2,1)S(1)}) all-reduce(f32[960]{0:T(1024)S(1)} %add.284, f32[960,320]{0,1:T(8,128)} %convolution_add_fusion.5, ...), channel_id=4, replica_groups=mesh['seq'=4,'dp'=8] {'dp'}, use_global_device_ids=true, to_apply=%region_18.19.clone | all-reduce | flops 616320 | bytes 3697920
  693.7 23.9 %reduce-scatter.31.cloned.1.call-done = f32[120,960]{1,0:T(8,128)} async-done(((f32[960,960]{1,0:T(8,128)}), f32[120,960]{1,0:T(8,128)}) %reduce-scatter.31.cloned.1.call-update) | async-done | bytes 460816 | tf_op jit(solution)/shard_map/reduce_scatter | solution.py:303
  719.5 51.8 %reduce-scatter.37.cloned.1.call-done = bf16[640,960]{1,0:T(8,128)(2,1)} async-done(((bf16[2560,960]{1,0:T(8,128)(2,1)}), bf16[640,960]{1,0:T(8,128)(2,1)}) %reduce-scatter.37.cloned.1.call-update) | async-done | bytes 1228816
  776.6 48.6 %reduce-scatter.39.cloned.1.call-done = bf16[640,960]{1,0:T(8,128)(2,1)} async-done(((bf16[2560,960]{1,0:T(8,128)(2,1)}), bf16[640,960]{1,0:T(8,128)(2,1)}) %reduce-scatter.39.cloned.1.call-update) | async-done | bytes 1228816
  830.6 48.6 %reduce-scatter.41.cloned.1.call-done = bf16[640,960]{1,0:T(8,128)(2,1)} async-done(((bf16[2560,960]{1,0:T(8,128)(2,1)}), bf16[640,960]{1,0:T(8,128)(2,1)}) %reduce-scatter.41.cloned.1.call-update) | async-done | bytes 1228816
  901.0 15.5 %all-reduce.14.cloned.1.call-done = (bf16[120,960]{1,0:T(8,128)(2,1)}, bf16[120,320]{0,1:T(8,128)(2,1)}, bf16[120,320]{0,1:T(8,128)(2,1)}, bf16[120,960]{1,0:T(8,128)(2,1)}) async-done(((bf16[120,960]{1,0:T(8,128)(2,1)}, bf16[120,320]{0,1:T(8,128)(2,1)}, bf16[120,320]{0,1:T(8,128)(2,1)}, bf16[120,960]{1,0:T(8,128)(2,1)}), (bf16[120,960]{1,0:T(8,128)(2,1)}, bf16[120,320]{0,1:T(8,128)(2,1)}, ...) | async-done | bytes 614416 | tf_op jit(solution)/shard_map/psum | solution.py:311
  923.2 67.8 %reduce-scatter.43.cloned.1.call-done = f32[120,640]{1,0:T(8,128)} async-done(((f32[960,640]{1,0:T(8,128)}), f32[120,640]{1,0:T(8,128)}) %reduce-scatter.43.cloned.1.call-update) | async-done | bytes 307216
  991.0 73.2 %reduce-scatter.45.cloned.1.call-done = f32[120,640]{1,0:T(8,128)} async-done(((f32[960,640]{1,0:T(8,128)}), f32[120,640]{1,0:T(8,128)}) %reduce-scatter.45.cloned.1.call-update) | async-done | bytes 307216
  1064.3 73.3 %reduce-scatter.47.cloned.1.call-done = f32[640,120]{0,1:T(8,128)} async-done(((f32[640,960]{0,1:T(8,128)}), f32[640,120]{0,1:T(8,128)}) %reduce-scatter.47.cloned.1.call-update) | async-done | bytes 307216
  (396 shorter events, 315.8 us)
Async XLA Ops:
  7.2 152.8 %copy-start = (bf16[960,960]{1,0:T(8,128)(2,1)S(1)}, bf16[960,960]{1,0:T(8,128)(2,1)}, u32[]{:S(2)}) copy-start(bf16[960,960]{1,0:T(8,128)(2,1)} %param.20) | copy-start | bytes 5529604
  7.2 108.8 %all-gather.5.cloned.1.call-start = ((), (), s32[]{:S(2)}) async-start(), calls=%async_computation.11 | async-start | bytes 2048000 | tf_op jit(solution)/shard_map/all_gather | solution.py:144
  9.3 19.6 %copy-start.76 = (f32[320]{0:T(512)}, f32[320]{0:T(512)S(1)}, u32[]{:S(2)}) copy-start(f32[320]{0:T(512)S(1)} %get-tuple-element.164) | copy-start | bytes 3844
  13.5 180.0 %copy-start.36 = (f32[320,32]{0,1:T(8,128)}, f32[320,32]{0,1:T(8,128)S(1)}, u32[]{:S(2)}) copy-start(f32[320,32]{0,1:T(8,128)S(1)} %get-tuple-element.162) | copy-start | bytes 122884
  14.7 154.0 %all-gather.7.cloned.1.call-start = ((), (), s32[]{:S(2)}) async-start(), calls=%async_computation.12 | async-start | bytes 6144000 | tf_op jit(solution)/shard_map/all_gather | solution.py:121
  19.3 144.1 %all-to-all-start = ((bf16[4,960,640]{2,1,0:T(8,128)(2,1)}), bf16[4,960,640]{2,1,0:T(8,128)(2,1)}, u32[]{:S(2)}, u32[]{:S(2)}) async-start(bf16[4,960,640]{2,1,0:T(8,128)(2,1)} %stack.2), calls=%async_computation | async-start | bytes 9830400 | tf_op jit(solution)/shard_map/all_to_all | solution.py:123
  24.2 156.1 %all-gather.9.cloned.1.call-start = ((), (), s32[]{:S(2)}) async-start(), calls=%async_computation.13 | async-start | bytes 6144000 | tf_op jit(solution)/shard_map/all_gather | solution.py:125
  25.0 185.8 %all-gather.11.cloned.1.call-start = ((), (), s32[]{:S(2)}) async-start(), calls=%async_computation.14 | async-start | bytes 2048000 | tf_op jit(solution)/shard_map/all_gather | solution.py:144
  190.7 174.7 %reduce-scatter.33.cloned.1.call-start = ((), (), s32[]{:S(2)}) async-start(), calls=%async_computation.17 | async-start | bytes 2048000
  303.5 16.4 %copy-start.41 = (bf16[1,320,15,32]{1,3,2,0:T(8,128)(2,1)S(1)}, bf16[1,320,15,32]{1,3,2,0:T(8,128)(2,1)}, u32[]{:S(2)}) copy-start(bf16[1,320,15,32]{1,3,2,0:T(8,128)(2,1)} %get-tuple-element.144) | copy-start | bytes 921604
  303.6 16.4 %copy-start.42 = (bf16[1,320,15,32]{1,3,2,0:T(8,128)(2,1)S(1)}, bf16[1,320,15,32]{1,3,2,0:T(8,128)(2,1)}, u32[]{:S(2)}) copy-start(bf16[1,320,15,32]{1,3,2,0:T(8,128)(2,1)} %get-tuple-element.145) | copy-start | bytes 921604
  336.7 201.9 %reduce-scatter.35.cloned.1.call-start = ((), (), s32[]{:S(2)}) async-start(), calls=%async_computation.18 | async-start | bytes 2048000
  347.1 28.7 %copy-start.48 = (bf16[1,320,15,64]{1,3,2,0:T(8,128)(2,1)}, bf16[1,320,15,64]{1,3,2,0:T(8,128)(2,1)S(1)}, u32[]{:S(2)}) copy-start(bf16[1,320,15,64]{1,3,2,0:T(8,128)(2,1)S(1)} %maximum_convert_fusion) | copy-start | bytes 1843204
  424.0 16.6 %copy-start.39 = (bf16[1,320,15,32]{1,3,2,0:T(8,128)(2,1)S(1)}, bf16[1,320,15,32]{1,3,2,0:T(8,128)(2,1)}, u32[]{:S(2)}) copy-start(bf16[1,320,15,32]{1,3,2,0:T(8,128)(2,1)} %get-tuple-element.146) | copy-start | bytes 921604
  424.0 16.6 %copy-start.40 = (bf16[1,320,15,32]{1,3,2,0:T(8,128)(2,1)S(1)}, bf16[1,320,15,32]{1,3,2,0:T(8,128)(2,1)}, u32[]{:S(2)}) copy-start(bf16[1,320,15,32]{1,3,2,0:T(8,128)(2,1)} %get-tuple-element.147) | copy-start | bytes 921604
  457.3 234.7 %reduce-scatter.29.cloned.1.call-start = ((), (), s32[]{:S(2)}) async-start(), calls=%async_computation.15 | async-start | bytes 4423680 | tf_op jit(solution)/shard_map/reduce_scatter | solution.py:300
  474.5 243.1 %reduce-scatter.31.cloned.1.call-start = ((), (), s32[]{:S(2)}) async-start(), calls=%async_computation.16 | async-start | bytes 4423680 | tf_op jit(solution)/shard_map/reduce_scatter | solution.py:303
  480.7 290.6 %reduce-scatter.37.cloned.1.call-start = ((), (), s32[]{:S(2)}) async-start(), calls=%async_computation.19 | async-start | bytes 6553600
  498.1 327.1 %reduce-scatter.39.cloned.1.call-start = ((), (), s32[]{:S(2)}) async-start(), calls=%async_computation.20 | async-start | bytes 6553600
  515.3 363.9 %reduce-scatter.41.cloned.1.call-start = ((), (), s32[]{:S(2)}) async-start(), calls=%async_computation.21 | async-start | bytes 6553600
  532.6 384.0 %all-reduce.14.cloned.1.call-start = ((), (), s32[]{:S(2)}) async-start(), calls=%async_computation.25 | async-start | bytes 1310720 | tf_op jit(solution)/shard_map/psum | solution.py:311
  719.5 271.6 %reduce-scatter.43.cloned.1.call-start = ((), (), s32[]{:S(2)}) async-start(), calls=%async_computation.22 | async-start | bytes 2764800
  776.6 287.7 %reduce-scatter.45.cloned.1.call-start = ((), (), s32[]{:S(2)}) async-start(), calls=%async_computation.23 | async-start | bytes 2764800
  830.5 307.0 %reduce-scatter.47.cloned.1.call-start = ((), (), s32[]{:S(2)}) async-start(), calls=%async_computation.24 | async-start | bytes 2764800
  (98 other events, 428.2 us)
Sparse Core Ops, SparseCore 0:
  14.8 30.8 all-gather.4
  47.3 64.0 all-gather.6
  113.0 38.5 all-gather.8
  190.8 19.8 all-gather.10
  336.8 28.5 reduce-scatter.32
  457.4 28.5 reduce-scatter.34
  489.8 89.2 reduce-scatter.28
  583.2 134.4 reduce-scatter.30
  720.2 51.0 reduce-scatter.36
  773.8 51.3 reduce-scatter.38
  827.8 51.3 reduce-scatter.40
  882.3 34.1 all-reduce.13
  921.2 69.7 reduce-scatter.42
  995.5 68.6 reduce-scatter.44
  1068.7 68.7 reduce-scatter.46
